TPU v7x, 256 devices: a whole 4x4x8 slice. The times are simulated.
256 devices in a mesh: blk: 64 (over x_hi, y, z), row: 4 (over x_lo, core).
Axes of the slice: x: 4 (x_hi: 2, x_lo: 2; x = x_hi * 2 + x_lo), y: 4, z: 8, core: 2. Of those that a mesh axis runs over, the one named last changes fastest.
Arguments:
- pool_embeds: bfloat16 [65536, 768], P('blk'), may hold values from -24 to 24
- target_samples: bfloat16 [16384, 768], P(('blk', 'row')), may hold values from -6 to 6
- reference_samples: bfloat16 [16384, 768], P(('blk', 'row')), may hold values from -6 to 6
Outputs:
- log_ratio: float32 [65536], P('blk')
- standardized: float32 [65536], P('blk')
All inputs are finite; a program needn't handle non-finite values.
Results may differ from a plain program's by a relative error of at most 0.0003.
Values may be sent and summed in bfloat16 or wider, within the bound.
No kernel may reach another device: no remote copies, remote signals or barrier semaphores. Data moves between devices by JAX's collectives and lax.ppermute only.
A program may use at most 128 MiB of HBM per device.

v0:
```python
import jax
import jax.numpy as jnp
from jax import lax
from jax.sharding import PartitionSpec as P

KERNEL_GAIN = 30.0


def make_fold(pool_rows):
    pool_norms = jnp.sum(jnp.square(pool_rows.astype(jnp.float32)), axis=1)
    factor = KERNEL_GAIN / pool_rows.shape[1]

    def fold(running, pieces, offset):
        width = pieces[0].shape[0]
        joined = jnp.concatenate([pieces[0], pieces[1]], axis=0)
        joined_norms = jnp.sum(jnp.square(joined.astype(jnp.float32)), axis=1)
        products = jnp.dot(pool_rows, joined.T, preferred_element_type=jnp.float32)
        scores_all = (2.0 * products - pool_norms[:, None] - joined_norms[None, :]) * factor
        result = []
        for member in range(2):
            highest = running[2 * member]
            total = running[2 * member + 1]
            scores = scores_all[:, member * width : (member + 1) * width]
            new_high = jnp.maximum(highest, jnp.max(scores, axis=1))
            new_total = jnp.sum(jnp.exp(scores - new_high[:, None]), axis=1)
            result.append(new_high)
            result.append(new_total)
        return tuple(result)

    return fold


def start_state(count):
    lowest = jnp.full((count,), -1e30, jnp.float32)
    nothing = jnp.zeros((count,), jnp.float32)
    return (lowest, nothing, lowest, nothing)


def body(pool_embeds, target_samples, reference_samples):
    pool_count = pool_embeds.shape[0]
    fold = make_fold(pool_embeds)
    state = fold(
        start_state(pool_count),
        (
            lax.all_gather(target_samples, "blk", axis=0, tiled=True),
            lax.all_gather(reference_samples, "blk", axis=0, tiled=True),
        ),
        jnp.int32(0),
    )
    high_target, high_ref = lax.pmax((state[0], state[2]), "row")
    total_target, total_ref = lax.psum(
        (state[1] * jnp.exp(state[0] - high_target), state[3] * jnp.exp(state[2] - high_ref)), "row"
    )
    log_ratio = high_target + jnp.log(total_target) - (high_ref + jnp.log(total_ref))
    whole_count = pool_count * lax.axis_size("blk")
    mean_value = lax.psum(jnp.sum(log_ratio), "blk") / whole_count
    variance = lax.psum(jnp.sum(jnp.square(log_ratio - mean_value)), "blk") / whole_count
    standardized = (log_ratio - mean_value) / jnp.sqrt(variance + 1e-05)
    return (log_ratio, standardized)


def solution(mesh):
    in_specs = (P("blk", None), P(("blk", "row"), None), P(("blk", "row"), None))
    out_specs = (P("blk"), P("blk"))
    return jax.shard_map(body, mesh=mesh, in_specs=in_specs, out_specs=out_specs, check_vma=False)
```

profile of v0, /device:TPU:32, one launch (start us, length us, event | category | flops | bytes accessed | tf_op | source)
XLA Modules:
  0.0 733.3 jit_solution(2255203302230212441)
XLA Ops:
  7.2 0.0 all-gather.3.cloned.1.call-start
  7.2 0.7 all-gather.3.cloned.1.call-update
  7.9 0.0 all-gather.5.cloned.1.call-start
  7.9 0.7 all-gather.5.cloned.1.call-update
  8.6 1.8 multiply_reduce_fusion.1
  10.4 0.0 copy-start.1
  10.4 141.4 %all-gather.3.cloned.1.call-done = bf16[4096,768]{1,0:T(8,128)(2,1)} async-done(((bf16[64,768]{1,0:T(8,128)(2,1)}), bf16[4096,768]{1,0:T(8,128)(2,1)}) %all-gather.3.cloned.1.call-update) | async-done | bytes 6291472 | tf_op jit(solution)/shard_map/all_gather | solution.py:45
  151.9 5.8 constant_dynamic-update-slice_fusion.1
  157.7 132.4 %all-gather.5.cloned.1.call-done = bf16[4096,768]{1,0:T(8,128)(2,1)} async-done(((bf16[64,768]{1,0:T(8,128)(2,1)}), bf16[4096,768]{1,0:T(8,128)(2,1)}) %all-gather.5.cloned.1.call-update) | async-done | bytes 6291472 | tf_op jit(solution)/shard_map/all_gather | solution.py:46
  290.1 5.8 constant_dynamic-update-slice_fusion
  295.9 7.1 multiply_reduce_fusion
  303.0 0.0 copy-done.1
  303.0 23.5 %multiply_bitcast_fusion = f32[1024,8192]{0,1:T(8,128)} fusion(bf16[8192,768]{1,0:T(8,128)(2,1)} %constant_dynamic-update-slice_fusion, bf16[1024,768]{1,0:T(8,128)(2,1)S(1)} %copy-done.1, f32[8192]{0:T(1024)S(1)} %multiply_reduce_fusion, f32[1024]{0:T(1024)S(1)} %multiply_reduce_fusion.1), kind=kOutput, calls=%fused_computation | convolution fusion | flops 12918456320 | bytes 47747072 | tf_op jit(solution)/shard_map/dot_general | solution.py:17
  326.5 0.0 copy-start
  326.5 11.7 %slice_reduce_fusion.1 = (f32[1024]{0:T(1024)S(1)}, f32[1024]{0:T(1024)S(1)}) fusion(f32[1024,8192]{0,1:T(8,128)} %multiply_bitcast_fusion), kind=kLoop, calls=%fused_computation.5 | loop fusion | flops 8386560 | bytes 33562624 | tf_op jit(solution)/shard_map/reduce_max | solution.py:24
  338.2 8.6 %copy-done = f32[1024,8192]{0,1:T(8,128)S(1)} copy-done((f32[1024,8192]{0,1:T(8,128)S(1)}, f32[1024,8192]{0,1:T(8,128)}, u32[]{:S(2)}) %copy-start) | copy-done | bytes 33554456
  346.7 4.5 exponential_reduce_fusion.1
  351.2 6.1 all-reduce.1
  357.4 5.9 all-reduce
  363.3 0.6 fusion
  363.9 0.0 copy-start.2
  363.9 177.7 %psum.30 = f32[]{:T(128)} all-reduce(f32[]{:T(128)} %get-tuple-element.10), channel_id=1, replica_groups=mesh['blk'=64,'row'=4] {'blk'}, use_global_device_ids=true, to_apply=%region_11.0 | all-reduce | flops 1 | bytes 8 | tf_op jit(solution)/shard_map/psum | solution.py:56
  542.3 0.6 multiply_reduce_fusion.2
  542.9 182.2 %psum.31 = f32[]{:T(128)} all-reduce(f32[]{:T(128)} %multiply_reduce_fusion.2), channel_id=1, replica_groups=mesh['blk'=64,'row'=4] {'blk'}, use_global_device_ids=true, to_apply=%region_13.0 | all-reduce | flops 1 | bytes 8 | tf_op jit(solution)/shard_map/psum | solution.py:57
  725.8 0.6 subtract_divide_fusion
  726.4 0.0 copy-done.2
  (3 shorter events, 0.0 us)
Async XLA Ops:
  7.2 144.7 %all-gather.3.cloned.1.call-start = ((), (), s32[]{:S(2)}) async-start(), calls=%async_computation | async-start | bytes 6389760 | tf_op jit(solution)/shard_map/all_gather | solution.py:45
  7.9 282.2 %all-gather.5.cloned.1.call-start = ((), (), s32[]{:S(2)}) async-start(), calls=%async_computation.1 | async-start | bytes 6389760 | tf_op jit(solution)/shard_map/all_gather | solution.py:46
  10.4 292.6 %copy-start.1 = (bf16[1024,768]{1,0:T(8,128)(2,1)S(1)}, bf16[1024,768]{1,0:T(8,128)(2,1)}, u32[]{:S(2)}) copy-start(bf16[1024,768]{1,0:T(8,128)(2,1)} %param.3) | copy-start | bytes 4718596
  326.5 20.3 %copy-start = (f32[1024,8192]{0,1:T(8,128)S(1)}, f32[1024,8192]{0,1:T(8,128)}, u32[]{:S(2)}) copy-start(f32[1024,8192]{0,1:T(8,128)} %multiply_bitcast_fusion) | copy-start | bytes 100663296
  363.9 362.5 %copy-start.2 = (f32[1024]{0:T(1024)}, f32[1024]{0:T(1024)S(1)}, u32[]{:S(2)}) copy-start(f32[1024]{0:T(1024)S(1)} %get-tuple-element.11) | copy-start | bytes 12292
Sparse Core Ops, SparseCore 0:
  11.7 140.1 all-gather.2
  155.6 134.4 all-gather.4
where the time goes:
time: 734 us; the launch traced here: 733 us
  blocking collectives  372 us (51%)
  waiting for transfers between devices  275 us (37%)
  other arithmetic  26.9 us (4%)
  matrix products  23.5 us (3%)
  local copies, waits for them, and re-layouts  20.2 us (3%)
  between operations  15.5 us (2%)
    psum x1, blocking collectives, body(): lax.psum(jnp.sum(jnp.square(log_ratio - mean_value)), 'blk') / whole_count  182 us
    psum x1, blocking collectives, body(): mean_value = lax.psum(jnp.sum(log_ratio), 'blk') / whole_count  178 us
    all_gather x1, waiting for transfers between devices, body(): lax.all_gather(target_samples, 'blk', axis=0, tiled=True)  141 us
    all_gather x1, waiting for transfers between devices, body(): lax.all_gather(reference_samples, 'blk', axis=0, tiled=True)  132 us
    dot_general x1, matrix products, fold(): products = jnp.dot(pool_rows, joined.T, preferred_element_type=jnp.float32)  23.5 us
  transfers between devices with their start and end apart: 2, of which 2 were waited for; matrix products, arithmetic and copies ran while one was open for 1% of the time, Pallas kernels for 0%

commit v1 on v0

--- a/solution.py
+++ b/solution.py
@@ -4,6 +4,11 @@
 from jax.sharding import PartitionSpec as P
 
 KERNEL_GAIN = 30.0
+
+
+def all_by_exchange(x, axis, dim):
+    sent = jnp.stack([x] * lax.axis_size(axis))
+    return jnp.concatenate(lax.all_to_all(sent, axis, 0, 0), axis=dim)
 
 
 def make_fold(pool_rows):
@@ -42,7 +47,7 @@
     state = fold(
         start_state(pool_count),
         (
-            lax.all_gather(target_samples, "blk", axis=0, tiled=True),
+            all_by_exchange(target_samples, "blk", 0),
             lax.all_gather(reference_samples, "blk", axis=0, tiled=True),
         ),
         jnp.int32(0),

time: 734 us -> 641 us (0.87)
  waiting for transfers between devices: 275 us -> 176 us
  starting transfers between devices: 0.08 us -> 14.4 us
    all_gather x1 -> x0, waiting for transfers between devices: 141 us -> none  [body(): lax.all_gather(target_samples, 'blk', axis=0, tiled=True)]
    all_gather x1, waiting for transfers between devices: 132 us -> 176 us  [body(): lax.all_gather(reference_samples, 'blk', axis=0, tiled=True)]
    all_to_all x0 -> x1, starting transfers between devices: none -> 14.4 us  [all_by_exchange(): return jnp.concatenate(lax.all_to_all(sent, axis, 0, 0), axis=dim)]
  transfers between devices with their start and end apart: 2 -> 2, of which waited for: 2 -> 1; matrix products, arithmetic and copies ran while one was open for 1% -> 1% of each run, Pallas kernels for 0% -> 0%
where the time goes in v1:
time: 641 us
  blocking collectives  370 us (58%)
  waiting for transfers between devices  176 us (27%)
  other arithmetic  27.9 us (4%)
  matrix products  23.1 us (4%)
  between operations  15.5 us (2%)
  starting transfers between devices  14.4 us (2%)
  local copies, waits for them, and re-layouts  12.9 us (2%)
    psum x1, blocking collectives, body(): lax.psum(jnp.sum(jnp.square(log_ratio - mean_value)), 'blk') / whole_count  182 us
    psum x1, blocking collectives, body(): mean_value = lax.psum(jnp.sum(log_ratio), 'blk') / whole_count  177 us
    all_gather x1, waiting for transfers between devices, body(): lax.all_gather(reference_samples, 'blk', axis=0, tiled=True)  176 us
    dot_general x1, matrix products, fold(): products = jnp.dot(pool_rows, joined.T, preferred_element_type=jnp.float32)  23.1 us
    all_to_all x1, starting transfers between devices, all_by_exchange(): return jnp.concatenate(lax.all_to_all(sent, axis, 0, 0), axis=dim)  14.4 us
  transfers between devices with their start and end apart: 2, of which 1 were waited for; matrix products, arithmetic and copies ran while one was open for 1% of the time, Pallas kernels for 0%

profile of v1, /device:TPU:32, one launch (start us, length us, event | category | flops | bytes accessed | tf_op | source)
XLA Modules:
  0.0 640.7 jit_solution(7529540277689439377)
XLA Ops:
  7.2 0.0 copy-start.1
  7.2 0.0 all-gather.2.cloned.1.call-start
  7.2 0.7 all-gather.2.cloned.1.call-update
  7.9 4.3 stack.2
  12.2 14.4 %all-to-all-start = ((bf16[64,64,768]{2,1,0:T(8,128)(2,1)}), bf16[64,64,768]{2,1,0:T(8,128)(2,1)}, u32[]{:S(2)}, u32[]{:S(2)}) async-start(bf16[64,64,768]{2,1,0:T(8,128)(2,1)} %stack.2), calls=%async_computation | async-start | bytes 12582912 | tf_op jit(solution)/shard_map/all_to_all | solution.py:11
  26.6 0.0 copy-done.1
  26.6 0.4 multiply_reduce_fusion.1
  27.0 175.8 %all-gather.2.cloned.1.call-done = bf16[4096,768]{1,0:T(8,128)(2,1)} async-done(((bf16[64,768]{1,0:T(8,128)(2,1)}), bf16[4096,768]{1,0:T(8,128)(2,1)}) %all-gather.2.cloned.1.call-update) | async-done | bytes 6291472 | tf_op jit(solution)/shard_map/all_gather | solution.py:51
  202.8 0.0 all-to-all-done
  202.8 9.5 %multiply_reduce_fusion = f32[8192]{0:T(1024)S(1)} fusion(bf16[4096,768]{1,0:T(8,128)(2,1)} %all-gather.2.cloned.1.call-done, bf16[4096,768]{1,0:T(8,128)(2,1)} %bitcast), kind=kLoop, calls=%fused_computation.1 | loop fusion | flops 37740544 | bytes 12615680 | tf_op jit(solution)/shard_map/reduce_sum | solution.py:21
  212.3 23.1 %multiply_bitcast_fusion = f32[1024,8192]{0,1:T(8,128)} fusion(bf16[1024,768]{1,0:T(8,128)(2,1)S(1)} %copy-done.1, f32[8192]{0:T(1024)S(1)} %multiply_reduce_fusion, f32[1024]{0:T(1024)S(1)} %multiply_reduce_fusion.1, bf16[4096,768]{1,0:T(8,128)(2,1)} %all-gather.2.cloned.1.call-done, bf16[4096,768]{1,0:T(8,128)(2,1)} %bitcast), kind=kOutput, calls=%fused_computation | convolution fusion | flops 12943622144 | bytes 47747072 | tf_op jit(solution)/shard_map/dot_general | solution.py:22
  235.4 0.0 copy-start
  235.4 11.7 %slice_reduce_fusion.1 = (f32[1024]{0:T(1024)S(1)}, f32[1024]{0:T(1024)S(1)}) fusion(f32[1024,8192]{0,1:T(8,128)} %multiply_bitcast_fusion), kind=kLoop, calls=%fused_computation.5 | loop fusion | flops 8386560 | bytes 33562624 | tf_op jit(solution)/shard_map/reduce_max | solution.py:29
  247.2 8.6 %copy-done = f32[1024,8192]{0,1:T(8,128)S(1)} copy-done((f32[1024,8192]{0,1:T(8,128)S(1)}, f32[1024,8192]{0,1:T(8,128)}, u32[]{:S(2)}) %copy-start) | copy-done | bytes 33554456
  255.7 4.5 exponential_reduce_fusion.1
  260.2 6.1 all-reduce.1
  266.3 5.9 all-reduce
  272.2 0.6 fusion.1
  272.8 0.0 copy-start.2
  272.8 176.7 %psum.30 = f32[]{:T(128)} all-reduce(f32[]{:T(128)} %get-tuple-element.10), channel_id=1, replica_groups=mesh['blk'=64,'row'=4] {'blk'}, use_global_device_ids=true, to_apply=%region_11.0 | all-reduce | flops 1 | bytes 8 | tf_op jit(solution)/shard_map/psum | solution.py:61
  450.1 0.6 multiply_reduce_fusion.2
  450.7 181.8 %psum.31 = f32[]{:T(128)} all-reduce(f32[]{:T(128)} %multiply_reduce_fusion.2), channel_id=1, replica_groups=mesh['blk'=64,'row'=4] {'blk'}, use_global_device_ids=true, to_apply=%region_13.0 | all-reduce | flops 1 | bytes 8 | tf_op jit(solution)/shard_map/psum | solution.py:62
  633.3 0.6 subtract_divide_fusion
  633.9 0.0 copy-done.2
  (3 shorter events, 0.0 us)
Async XLA Ops:
  7.2 19.5 %copy-start.1 = (bf16[1024,768]{1,0:T(8,128)(2,1)S(1)}, bf16[1024,768]{1,0:T(8,128)(2,1)}, u32[]{:S(2)}) copy-start(bf16[1024,768]{1,0:T(8,128)(2,1)} %param.3) | copy-start | bytes 4718596
  7.2 195.6 %all-gather.2.cloned.1.call-start = ((), (), s32[]{:S(2)}) async-start(), calls=%async_computation.1 | async-start | bytes 6389760 | tf_op jit(solution)/shard_map/all_gather | solution.py:51
  12.2 190.6 %all-to-all-start = ((bf16[64,64,768]{2,1,0:T(8,128)(2,1)}), bf16[64,64,768]{2,1,0:T(8,128)(2,1)}, u32[]{:S(2)}, u32[]{:S(2)}) async-start(bf16[64,64,768]{2,1,0:T(8,128)(2,1)} %stack.2), calls=%async_computation | async-start | bytes 12582912 | tf_op jit(solution)/shard_map/all_to_all | solution.py:11
  235.4 20.3 %copy-start = (f32[1024,8192]{0,1:T(8,128)S(1)}, f32[1024,8192]{0,1:T(8,128)}, u32[]{:S(2)}) copy-start(f32[1024,8192]{0,1:T(8,128)} %multiply_bitcast_fusion) | copy-start | bytes 100663296
  272.8 361.1 %copy-start.2 = (f32[1024]{0:T(1024)}, f32[1024]{0:T(1024)S(1)}, u32[]{:S(2)}) copy-start(f32[1024]{0:T(1024)S(1)} %get-tuple-element.11) | copy-start | bytes 12292
Sparse Core Ops, SparseCore 0:
  11.7 191.1 all-gather.1
